TPU v7x, 32 devices: a whole 2x2x4 slice. The times are simulated.
32 devices in a mesh: groups: 1, role: 2 (over core), ep: 8 (over z, y), tp: 2 (over x).
Axes of the slice: x: 2, y: 2, z: 4, core: 2. Of those that a mesh axis runs over, the one named last changes fastest.
Arguments:
- tokens: bfloat16 [2048, 2048], P(('groups', 'role', 'ep'), 'tp'), may hold values from -6 to 6
- out_grad: bfloat16 [2048, 2048], P(('groups', 'role', 'ep'), 'tp'), may hold values from -6 to 6
- routes: int32 [2048, 8], P(('groups', 'role', 'ep')), may hold values from 0 to 15, all different within a row; in each aligned block of 128 rows (0 to 127, 128 to 255, ...) at most 72 rows name the same one
- probs: bfloat16 [2048, 8], P(('groups', 'role', 'ep')), may hold values from 0.049804688 to 1
- w_gate: bfloat16 [16, 2048, 768], P(('role', 'ep'), None, 'tp'), may hold values from -0.125 to 0.125
- w_up: bfloat16 [16, 2048, 768], P(('role', 'ep'), None, 'tp'), may hold values from -0.125 to 0.125
- w_down: bfloat16 [16, 768, 2048], P(('role', 'ep'), 'tp'), may hold values from -0.21875 to 0.21875
Outputs:
- d_tokens: bfloat16 [2048, 2048], P(('groups', 'role', 'ep'), 'tp')
- d_probs: float32 [2048, 8], P(('groups', 'role', 'ep'))
- d_w_gate: bfloat16 [16, 2048, 768], P(('groups', 'role', 'ep'), None, 'tp')
- d_w_up: bfloat16 [16, 2048, 768], P(('groups', 'role', 'ep'), None, 'tp')
- d_w_down: bfloat16 [16, 768, 2048], P(('groups', 'role', 'ep'), 'tp')
Inputs may be any that keep to these rules, and one draw needn't show every extreme that they name: `routes`: in each aligned block of 128 rows (the tokens of one index of role and ep) no expert is named by more than 72 rows, a bound that some block reaches.
All inputs are finite; a program needn't handle non-finite values.
Results may differ from a plain program's by a relative error of at most 0.012.
Values may be sent and summed in bfloat16 or wider, within the bound.
A program may use at most 128 MiB of HBM per device.

v0:
```python
import jax
import jax.numpy as jnp
from jax import lax
from jax.sharding import PartitionSpec as P


def pad_rows(array):
    return jnp.concatenate([array, jnp.zeros((1, array.shape[1]), array.dtype)], 0)


def per_device(tokens, out_grad, routes, probs, w_gate, w_up, w_down):
    owners = lax.axis_size(("role", "ep"))
    tok_rows, top_count = routes.shape
    width_full = w_gate.shape[1]
    part_width = w_gate.shape[2]
    capacity = min(tok_rows, tok_rows * top_count * 9 // (8 * owners))
    entry_total = tok_rows * top_count
    routes_flat = routes.reshape(-1)
    onehot = (routes_flat[:, None] == jnp.arange(owners, dtype=jnp.int32)[None, :]).astype(
        jnp.int32
    )
    before = jnp.cumsum(onehot, axis=0) - onehot
    slot_index = jnp.sum(before * onehot, axis=1)
    target = routes_flat * capacity + slot_index
    row_count = owners * capacity
    entry_of_slot = (
        jnp.full((row_count,), entry_total, jnp.int32)
        .at[target]
        .set(jnp.arange(entry_total, dtype=jnp.int32))
    )
    token_of_slot = entry_of_slot // top_count
    padded_prob = jnp.concatenate([probs.reshape(-1), jnp.zeros((1,), probs.dtype)], 0)
    send_prob = padded_prob[entry_of_slot].reshape(owners, capacity)
    send_x = pad_rows(tokens)[token_of_slot]
    send_g = pad_rows(out_grad)[token_of_slot]
    slice_x, slice_g, recv_p = (
        lax.all_to_all(
            send_x.reshape(owners, capacity, tokens.shape[1]),
            ("role", "ep"),
            split_axis=0,
            concat_axis=0,
            tiled=True,
        ),
        lax.all_to_all(
            send_g.reshape(owners, capacity, tokens.shape[1]),
            ("role", "ep"),
            split_axis=0,
            concat_axis=0,
            tiled=True,
        ),
        lax.all_to_all(send_prob, ("role", "ep"), split_axis=0, concat_axis=0, tiled=True),
    )
    recv_x, recv_g = (
        lax.all_gather(slice_x, "tp", axis=2, tiled=True),
        lax.all_gather(slice_g, "tp", axis=2, tiled=True),
    )
    rows_x = recv_x.reshape(row_count, width_full)
    rows_g = recv_g.reshape(row_count, width_full)
    weight_p = recv_p.reshape(row_count, 1).astype(jnp.float32)
    gate_up = jnp.concatenate([w_gate[0], w_up[0]], 1)
    down_shard = w_down[0]
    both_rows = jnp.dot(rows_x, gate_up, preferred_element_type=jnp.float32)
    gate_rows = both_rows[:, :part_width]
    up_rows = both_rows[:, part_width:]
    sigmoid_gate = jax.nn.sigmoid(gate_rows)
    activated = gate_rows * sigmoid_gate
    hidden = activated * up_rows
    back_rows = lax.dot_general(
        rows_g, down_shard, (((1,), (1,)), ((), ())), preferred_element_type=jnp.float32
    )
    scores = lax.psum(jnp.sum(hidden * back_rows, axis=1), "tp")
    hidden_grad = weight_p * back_rows
    d_gate_rows = (
        hidden_grad * up_rows * sigmoid_gate * (1.0 + gate_rows * (1.0 - sigmoid_gate))
    ).astype(jnp.bfloat16)
    d_up_rows = (hidden_grad * activated).astype(jnp.bfloat16)
    d_both = jnp.concatenate([d_gate_rows, d_up_rows], 1)
    scaled = (weight_p * hidden).astype(jnp.bfloat16)
    grad_down = lax.dot_general(
        scaled, rows_g, (((0,), (0,)), ((), ())), preferred_element_type=jnp.float32
    )
    grad_both = lax.dot_general(
        rows_x, d_both, (((0,), (0,)), ((), ())), preferred_element_type=jnp.float32
    )
    grad_gate = grad_both[:, :part_width]
    grad_up = grad_both[:, part_width:]
    partial_low = lax.dot_general(
        d_both, gate_up, (((1,), (1,)), ((), ())), preferred_element_type=jnp.float32
    ).astype(jnp.bfloat16)
    home_s = lax.all_to_all(
        scores.reshape(owners, capacity), ("role", "ep"), split_axis=0, concat_axis=0, tiled=True
    )
    summed = lax.psum_scatter(
        partial_low.reshape(owners, capacity, width_full), "tp", scatter_dimension=2, tiled=True
    ).astype(jnp.float32)
    summed_low = summed.astype(jnp.bfloat16)
    home_x = lax.all_to_all(summed_low, ("role", "ep"), split_axis=0, concat_axis=0, tiled=True)
    slice_width = summed.shape[2]
    route_rows = home_x.reshape(row_count, slice_width).astype(jnp.float32)
    d_tok = (
        jnp.zeros((tok_rows + 1, slice_width), jnp.float32)
        .at[token_of_slot]
        .add(route_rows)[:tok_rows]
    )
    d_probs = home_s.reshape(-1)[target].reshape(tok_rows, top_count)
    return (
        d_tok.astype(jnp.bfloat16),
        d_probs,
        grad_gate.astype(jnp.bfloat16)[None],
        grad_up.astype(jnp.bfloat16)[None],
        grad_down.astype(jnp.bfloat16)[None],
    )


def solution(mesh):
    in_specs = (
        P(("groups", "role", "ep"), "tp"),
        P(("groups", "role", "ep"), "tp"),
        P(("groups", "role", "ep"), None),
        P(("groups", "role", "ep"), None),
        P(("role", "ep"), None, "tp"),
        P(("role", "ep"), None, "tp"),
        P(("role", "ep"), "tp", None),
    )
    out_specs = (
        P(("groups", "role", "ep"), "tp"),
        P(("groups", "role", "ep"), None),
        P(("groups", "role", "ep"), None, "tp"),
        P(("groups", "role", "ep"), None, "tp"),
        P(("groups", "role", "ep"), "tp", None),
    )
    return jax.shard_map(
        per_device, mesh=mesh, in_specs=in_specs, out_specs=out_specs, check_vma=False
    )
```

profile of v0, /device:TPU:0, one launch (start us, length us, event | category | flops | bytes accessed | tf_op | source)
XLA Modules:
  0.0 366.0 jit_solution(3342782884633505254)
XLA Ops:
  7.2 0.0 copy-start
  7.2 0.0 all-gather.5.cloned.1.call-start
  7.2 0.8 broadcast_multiply_fusion
  8.0 0.8 copy.22
  8.8 0.1 eq.29
  8.9 0.1 eq.25
  9.0 0.1 copy.21
  9.1 0.1 mul.59
  9.2 4.5 %reduce-window.6 = s32[16,8,128]{2,1,0:T(8,128)S(1)} reduce-window(s32[16,8,128]{2,1,0:T(8,128)S(1)} %fusion.12, s32[]{:T(128)} %constant.17.clone.1), window={size=1x1x128 pad=0_0x0_0x127_0}, to_apply=%region_0.0 | reduce-window | flops 2080768 | bytes 131076 | tf_op jit(solution)/shard_map/reduce-window
  13.7 0.1 slice.39
  13.8 0.1 copy.24
  14.0 0.1 copy.25
  14.0 0.1 broadcast_add_fusion
  14.2 4.3 %scatter_custom_fusion = s32[1152]{0:T(1024)S(1)} fusion(s32[1024]{0:T(1024)S(1)} %bitcast.51, s32[1024]{0:T(1024)S(1)} %iota.11, s32[]{:T(128)} %constant.11.clone.1), kind=kCustom, calls=%fused_computation.51 | custom fusion | bytes 4612 | tf_op jit(solution)/shard_map/scatter | solution.py:29
  18.6 1.0 concatenate.17
  19.5 5.0 %gather_fusion.2 = bf16[1152,1024]{1,0:T(8,128)(2,1)} fusion(bf16[129,1024]{1,0:T(8,128)(2,1)S(1)} %concatenate.17, s32[2048]{0:T(1024)S(1)} %get-tuple-element.22), kind=kCustom, calls=%fused_computation.2 | custom fusion | bytes 4723200 | tf_op jit(solution)/shard_map/gather | solution.py:34
  24.6 62.8 %all_to_all.34 = bf16[16,72,1024]{2,1,0:T(8,128)(2,1)} all-to-all(bf16[16,72,1024]{2,1,0:T(8,128)(2,1)} %bitcast.46), channel_id=1, replica_groups=mesh['groups'=1,'role'=2,'ep'=8,'tp'=2] {'role','ep'}, dimensions={0} | all-to-all | bytes 4718592 | tf_op jit(solution)/shard_map/all_to_all | solution.py:37
  87.4 0.0 all-gather.5.cloned.1.call-update
  87.4 0.0 all-gather.3.cloned.1.call-start
  87.4 0.9 copy-done.1
  88.3 5.0 %gather_fusion.1 = bf16[1152,1024]{1,0:T(8,128)(2,1)} fusion(bf16[129,1024]{1,0:T(8,128)(2,1)S(1)} %concatenate.16, s32[2048]{0:T(1024)S(1)} %get-tuple-element.22), kind=kCustom, calls=%fused_computation.1 | custom fusion | bytes 4723200 | tf_op jit(solution)/shard_map/gather | solution.py:35
  93.4 59.7 %all_to_all.35 = bf16[16,72,1024]{2,1,0:T(8,128)(2,1)} all-to-all(bf16[16,72,1024]{2,1,0:T(8,128)(2,1)} %bitcast.45), channel_id=1, replica_groups=mesh['groups'=1,'role'=2,'ep'=8,'tp'=2] {'role','ep'}, dimensions={0} | all-to-all | bytes 4718592 | tf_op jit(solution)/shard_map/all_to_all | solution.py:44
  153.1 0.0 all-gather.3.cloned.1.call-update
  153.1 0.0 copy-start.3
  153.1 0.0 reduce-scatter.2.cloned.1.call-start
  153.2 0.6 copy-done.2
  153.8 0.1 copy.26
  153.9 0.1 reshape.104
  154.0 7.2 %gather_fusion = bf16[1152]{0:T(1024)(128)(2,1)S(1)} fusion(bf16[1025]{0:T(1024)(128)(2,1)S(1)} %pad_maximum_fusion.6, s32[2048]{0:T(1024)S(1)} %get-tuple-element.23), kind=kCustom, calls=%fused_computation | custom fusion | bytes 9216 | tf_op jit(solution)/shard_map/gather | solution.py:33
  161.3 0.1 all_to_all.28
  161.4 8.9 %all_to_all.36 = bf16[16,1,72]{2,1,0:T(2,128)(2,1)S(1)} all-to-all(bf16[16,1,72]{2,1,0:T(2,128)(2,1)S(1)} %all_to_all.28), channel_id=1, replica_groups=mesh['groups'=1,'role'=2,'ep'=8,'tp'=2] {'role','ep'}, dimensions={0} | all-to-all | bytes 4608 | tf_op jit(solution)/shard_map/all_to_all | solution.py:51
  170.3 0.1 reshape.112
  170.4 0.0 all-gather.5.cloned.1.call-done
  170.4 0.0 copy-done.3
  170.5 8.9 %fusion.3 = f32[1152,768]{0,1:T(8,128)} fusion(bf16[1152,2048]{1,0:T(8,128)(2,1)} %bitcast.53, bf16[2048,384]{1,0:T(8,128)(2,1)S(1)} %bitcast.57, bf16[2048,384]{1,0:T(8,128)(2,1)} %bitcast.59), kind=kOutput, calls=%fused_computation.13 | convolution fusion | flops 3630170112 | bytes 11403264 | tf_op jit(solution)/shard_map/dot_general | solution.py:62
  179.4 34.5 %all-gather.3.cloned.1.call-done = bf16[16,72,2048]{2,1,0:T(8,128)(2,1)} async-done(((bf16[16,72,1024]{2,1,0:T(8,128)(2,1)}), bf16[16,72,2048]{2,1,0:T(8,128)(2,1)}) %all-gather.3.cloned.1.call-update) | async-done | bytes 4718608 | tf_op jit(solution)/shard_map/all_gather | solution.py:55
  213.8 0.0 copy-done
  213.8 6.3 %multiply_convert_fusion.2 = (bf16[1152,384]{0,1:T(8,128)(2,1)S(1)}, bf16[1152,384]{0,1:T(8,128)(2,1)S(1)}, f32[1152]{0:T(1024)S(1)}) fusion(f32[1152,768]{0,1:T(8,128)} %fusion.3, f32[1152]{0:T(1024)S(1)} %reshape.112, bf16[1152,2048]{1,0:T(8,128)(2,1)} %bitcast.55, bf16[1,384,2048]{2,1,0:T(8,128)(2,1)S(1)} %copy-done), kind=kOutput, calls=%fused_computation.18 | convolution fusion | flops 1819458432 | bytes 11609088 | tf_op jit(solution)/shard_map/dot_general | solution.py:68
  220.1 0.0 copy-start.6
  220.2 0.0 copy-start.8
  220.2 0.0 copy-done.4
  220.2 5.6 %convolution_convert_fusion = bf16[1152,2048]{1,0:T(8,128)(2,1)} fusion(bf16[2048,384]{1,0:T(8,128)(2,1)S(1)} %bitcast.58, bf16[2048,384]{1,0:T(8,128)(2,1)S(1)} %bitcast.60, bf16[1152,384]{0,1:T(8,128)(2,1)S(1)} %get-tuple-element.16, bf16[1152,384]{0,1:T(8,128)(2,1)S(1)} %get-tuple-element.15), kind=kOutput, calls=%fused_computation.6 | convolution fusion | flops 3636068352 | bytes 9633792 | tf_op jit(solution)/shard_map/dot_general | solution.py:87
  225.8 0.0 copy-done.6
  225.8 0.0 reduce-scatter.2.cloned.1.call-update
  225.8 0.1 all_to_all.26
  225.9 5.0 %psum.7 = f32[16,1,72]{2,1,0:T(1,128)S(1)} all-reduce(f32[16,1,72]{2,1,0:T(1,128)S(1)} %all_to_all.26), channel_id=1, replica_groups=mesh['groups'=1,'role'=2,'ep'=8,'tp'=2] {'tp'}, use_global_device_ids=true, to_apply=%region_7.8 | all-reduce | flops 1152 | bytes 9216 | tf_op jit(solution)/shard_map/psum | solution.py:71
  230.9 11.8 %all_to_all.37 = f32[16,1,72]{2,1,0:T(1,128)S(1)} all-to-all(f32[16,1,72]{2,1,0:T(1,128)S(1)} %psum.7), channel_id=1, replica_groups=mesh['groups'=1,'role'=2,'ep'=8,'tp'=2] {'role','ep'}, dimensions={0} | all-to-all | bytes 9216 | tf_op jit(solution)/shard_map/all_to_all | solution.py:90
  242.8 43.3 %reduce-scatter.2.cloned.1.call-done = bf16[16,72,1024]{2,1,0:T(8,128)(2,1)} async-done(((bf16[16,72,2048]{2,1,0:T(8,128)(2,1)}), bf16[16,72,1024]{2,1,0:T(8,128)(2,1)}) %reduce-scatter.2.cloned.1.call-update) | async-done | bytes 2359312 | tf_op jit(solution)/shard_map/reduce_scatter | solution.py:93
  286.1 5.7 %all-to-all-start.3 = ((bf16[16,72,1024]{2,1,0:T(8,128)(2,1)}), bf16[16,72,1024]{2,1,0:T(8,128)(2,1)}, u32[]{:S(2)}, u32[]{:S(2)}) async-start(bf16[16,72,1024]{2,1,0:T(8,128)(2,1)} %reduce-scatter.2.cloned.1.call-done), calls=%async_computation.4 | async-start | bytes 4718592 | tf_op jit(solution)/shard_map/all_to_all | solution.py:97
  291.8 0.0 copy-done.7
  291.8 0.0 copy-done.9
  291.8 7.8 %convolution_convert_fusion.1 = bf16[2048,768]{1,0:T(8,128)(2,1)S(1)} fusion(bf16[1152,2048]{1,0:T(8,128)(2,1)} %bitcast.54, bf16[1152,384]{0,1:T(8,128)(2,1)S(1)} %copy-done.9, bf16[1152,384]{0,1:T(8,128)(2,1)S(1)} %copy-done.7), kind=kOutput, calls=%fused_computation.9 | convolution fusion | flops 3628990464 | bytes 9633792 | tf_op jit(solution)/shard_map/dot_general | solution.py:82
  299.6 2.0 slice_bitcast_fusion
  301.6 1.2 copy-done.5
  302.7 5.7 %fusion.2 = bf16[1,384,2048]{2,1,0:T(8,128)(2,1)} fusion(bf16[1152,2048]{1,0:T(8,128)(2,1)} %bitcast.56, f32[1152]{0:T(1024)S(1)} %reshape.112, f32[1152,768]{0,1:T(8,128)S(1)} %copy-done.5), kind=kOutput, calls=%fused_computation.12 | convolution fusion | flops 1815822336 | bytes 9835008 | tf_op jit(solution)/shard_map/dot_general | solution.py:79
  308.5 0.5 broadcast.105
  309.0 0.7 reduce.7
  309.7 0.1 reshape.110
  309.8 6.2 %gather_fusion.3 = f32[1024]{0:T(1024)S(1)} fusion(f32[1152]{0:T(1024)S(1)} %reshape.110, s32[1024]{0:T(1024)S(1)} %broadcast_clamp_fusion), kind=kCustom, calls=%fused_computation.3 | custom fusion | bytes 12288 | tf_op jit(solution)/shard_map/gather | solution.py:105
  315.9 0.1 reshape.111
  316.0 0.7 copy.28
  316.7 28.0 %all-to-all-done.3 = bf16[16,72,1024]{2,1,0:T(8,128)(2,1)} async-done(((bf16[16,72,1024]{2,1,0:T(8,128)(2,1)}), bf16[16,72,1024]{2,1,0:T(8,128)(2,1)}, u32[]{:S(2)}, u32[]{:S(2)}) %all-to-all-start.3) | async-done | bytes 2359328 | tf_op jit(solution)/shard_map/all_to_all | solution.py:97
  344.7 14.0 %scatter_custom_fusion.1 = f32[129,1024]{1,0:T(8,128)S(1)} fusion(s32[1152]{0:T(1024)S(1)} %get-tuple-element.21, bf16[1152,1024]{1,0:T(8,128)(2,1)} %bitcast.16, f32[]{:T(128)} %constant.14.clone.1), kind=kCustom, calls=%fused_computation.7 | custom fusion | flops 2359296 | bytes 2887684 | tf_op jit(solution)/shard_map/scatter-add | solution.py:103
  358.7 0.7 slice.65
  (19 shorter events, 0.2 us)
Async XLA Ops:
  7.2 206.7 %copy-start = (bf16[1,384,2048]{2,1,0:T(8,128)(2,1)S(1)}, bf16[1,384,2048]{2,1,0:T(8,128)(2,1)}, u32[]{:S(2)}) copy-start(bf16[1,384,2048]{2,1,0:T(8,128)(2,1)} %param.13) | copy-start | bytes 4718596
  7.2 163.3 %all-gather.5.cloned.1.call-start = ((), (), s32[]{:S(2)}) async-start(), calls=%async_computation.7 | async-start | bytes 7077888 | tf_op jit(solution)/shard_map/all_gather | solution.py:54
  87.4 1.0 copy-start.1
  87.4 126.5 %all-gather.3.cloned.1.call-start = ((), (), s32[]{:S(2)}) async-start(), calls=%async_computation.6 | async-start | bytes 7077888 | tf_op jit(solution)/shard_map/all_gather | solution.py:55
  153.1 0.7 copy-start.2
  153.1 17.3 %copy-start.3 = (bf16[1,2048,384]{2,1,0:T(8,128)(2,1)S(1)}, bf16[1,2048,384]{2,1,0:T(8,128)(2,1)}, u32[]{:S(2)}) copy-start(bf16[1,2048,384]{2,1,0:T(8,128)(2,1)} %param.12) | copy-start | bytes 4718596
  153.1 132.9 %reduce-scatter.2.cloned.1.call-start = ((), (), s32[]{:S(2)}) async-start(), calls=%async_computation.8 | async-start | bytes 7077888 | tf_op jit(solution)/shard_map/reduce_scatter | solution.py:93
  213.8 6.3 %copy-start.4 = (bf16[1,2048,384]{2,1,0:T(8,128)(2,1)S(1)}, bf16[1,2048,384]{2,1,0:T(8,128)(2,1)}, u32[]{:S(2)}) copy-start(bf16[1,2048,384]{2,1,0:T(8,128)(2,1)} %param.11) | copy-start | bytes 4718596
  220.1 5.7 %copy-start.6 = (bf16[1152,384]{0,1:T(8,128)(2,1)}, bf16[1152,384]{0,1:T(8,128)(2,1)S(1)}, u32[]{:S(2)}) copy-start(bf16[1152,384]{0,1:T(8,128)(2,1)S(1)} %get-tuple-element.15) | copy-start | bytes 2654212
  220.2 5.6 %copy-start.8 = (bf16[1152,384]{0,1:T(8,128)(2,1)}, bf16[1152,384]{0,1:T(8,128)(2,1)S(1)}, u32[]{:S(2)}) copy-start(bf16[1152,384]{0,1:T(8,128)(2,1)S(1)} %get-tuple-element.16) | copy-start | bytes 2654212
  242.8 49.0 %copy-start.7 = (bf16[1152,384]{0,1:T(8,128)(2,1)S(1)}, bf16[1152,384]{0,1:T(8,128)(2,1)}, u32[]{:S(2)}) copy-start(bf16[1152,384]{0,1:T(8,128)(2,1)} %copy-done.6) | copy-start | bytes 2654212
  242.8 49.0 %copy-start.9 = (bf16[1152,384]{0,1:T(8,128)(2,1)S(1)}, bf16[1152,384]{0,1:T(8,128)(2,1)}, u32[]{:S(2)}) copy-start(bf16[1152,384]{0,1:T(8,128)(2,1)} %copy-done.8) | copy-start | bytes 2654212
  286.1 58.6 %all-to-all-start.3 = ((bf16[16,72,1024]{2,1,0:T(8,128)(2,1)}), bf16[16,72,1024]{2,1,0:T(8,128)(2,1)}, u32[]{:S(2)}, u32[]{:S(2)}) async-start(bf16[16,72,1024]{2,1,0:T(8,128)(2,1)} %reduce-scatter.2.cloned.1.call-done), calls=%async_computation.4 | async-start | bytes 4718592 | tf_op jit(solution)/shard_map/all_to_all | solution.py:97
  299.6 3.1 copy-start.5
Sparse Core Ops, SparseCore 0:
  87.5 60.5 all-gather.4
  153.2 60.5 all-gather.2
  225.9 60.0 reduce-scatter.1
where the time goes:
time: 367 us; the launch traced here: 366 us
  blocking collectives  148 us (40%)
  waiting for transfers between devices  106 us (29%)
  local copies, waits for them, and re-layouts  37.4 us (10%)
  matrix products  34.4 us (9%)
  other arithmetic  20.2 us (6%)
  between operations  14 us (4%)
  starting transfers between devices  5.78 us (2%)
    all_to_all x1, blocking collectives, per_device(): lax.all_to_all(send_x.reshape(owners, capacity, tokens.shape[1]), ('role'...  62.8 us
    all_to_all x1, blocking collectives, per_device(): lax.all_to_all(send_g.reshape(owners, capacity, tokens.shape[1]), ('role'...  59.7 us
    reduce_scatter x1, waiting for transfers between devices, per_device(): lax.psum_scatter(partial_low.reshape(owners, capacity, width_full), 'tp',...  43.3 us
    all_gather x1, waiting for transfers between devices, per_device(): lax.all_gather(slice_g, 'tp', axis=2, tiled=True)  34.5 us
    all_to_all x1, waiting for transfers between devices, per_device(): lax.all_to_all(summed_low, ('role', 'ep'), split_axis=0, concat_axis=0, t...  28 us
    scatter-add x1, other arithmetic, per_device(): d_tok = jnp.zeros((tok_rows + 1, slice_width), jnp.float32).at[token_of_s...  14 us
    all_to_all x1, blocking collectives, per_device(): lax.all_to_all(scores.reshape(owners, capacity), ('role', 'ep'), split_ax...  11.8 us
    all_to_all x1, blocking collectives, per_device(): lax.all_to_all(send_prob, ('role', 'ep'), split_axis=0, concat_axis=0, ti...  8.94 us
  transfers between devices with their start and end apart: 4, of which 3 were waited for; matrix products, arithmetic and copies ran while one was open for 12% of the time, Pallas kernels for 0%

commit v1 on v0

--- a/solution.py
+++ b/solution.py
@@ -8,7 +8,7 @@
     return jnp.concatenate([array, jnp.zeros((1, array.shape[1]), array.dtype)], 0)
 
 
-def per_device(tokens, out_grad, routes, probs, w_gate, w_up, w_down):
+def routed_device(tokens, out_grad, routes, probs, w_gate, w_up, w_down):
     owners = lax.axis_size(("role", "ep"))
     tok_rows, top_count = routes.shape
     width_full = w_gate.shape[1]
@@ -112,6 +112,76 @@
     )
 
 
+def dense_device(tokens, out_grad, routes, probs, w_gate, w_up, w_down):
+    owners = lax.axis_size(("role", "ep"))
+    tok_rows, top_count = routes.shape
+    part_width = w_gate.shape[2]
+    experts = jnp.arange(owners, dtype=jnp.int32)
+    chosen = routes[:, :, None] == experts[None, None, :]
+    prob_table = jnp.sum(
+        jnp.where(chosen, probs[:, :, None].astype(jnp.float32), 0.0), axis=1
+    )
+    send_p = prob_table.T.astype(jnp.bfloat16).reshape(owners, 1, tok_rows)
+    recv_p = lax.all_to_all(send_p, ("role", "ep"), split_axis=0, concat_axis=0, tiled=True)
+    weight_p = recv_p.reshape(owners * tok_rows, 1).astype(jnp.float32)
+    rows_x = gather_rows(tokens)
+    rows_g = gather_rows(out_grad)
+    gate_up = jnp.concatenate([w_gate[0], w_up[0]], 1)
+    down_shard = w_down[0]
+    both_rows = jnp.dot(rows_x, gate_up, preferred_element_type=jnp.float32)
+    gate_rows = both_rows[:, :part_width]
+    up_rows = both_rows[:, part_width:]
+    sigmoid_gate = jax.nn.sigmoid(gate_rows)
+    activated = gate_rows * sigmoid_gate
+    hidden = activated * up_rows
+    back_rows = lax.dot_general(
+        rows_g, down_shard, (((1,), (1,)), ((), ())), preferred_element_type=jnp.float32
+    )
+    scores = jnp.sum(hidden * back_rows, axis=1)
+    hidden_grad = weight_p * back_rows
+    d_gate_rows = (
+        hidden_grad * up_rows * sigmoid_gate * (1.0 + gate_rows * (1.0 - sigmoid_gate))
+    ).astype(jnp.bfloat16)
+    d_up_rows = (hidden_grad * activated).astype(jnp.bfloat16)
+    d_both = jnp.concatenate([d_gate_rows, d_up_rows], 1)
+    scaled = (weight_p * hidden).astype(jnp.bfloat16)
+    partial_low = lax.dot_general(
+        d_both, gate_up, (((1,), (1,)), ((), ())), preferred_element_type=jnp.float32
+    ).astype(jnp.bfloat16)
+    summed = lax.psum_scatter(partial_low, ("role", "ep"), scatter_dimension=0, tiled=True)
+    d_tok = lax.psum_scatter(summed, "tp", scatter_dimension=1, tiled=True)
+    grad_down = lax.dot_general(
+        scaled, rows_g, (((0,), (0,)), ((), ())), preferred_element_type=jnp.float32
+    )
+    grad_both = lax.dot_general(
+        rows_x, d_both, (((0,), (0,)), ((), ())), preferred_element_type=jnp.float32
+    )
+    home_s = lax.all_to_all(
+        scores.reshape(owners, 1, tok_rows), ("role", "ep"), split_axis=0, concat_axis=0, tiled=True
+    )
+    home_s = lax.psum(home_s, "tp").reshape(owners, tok_rows).T
+    d_probs = jnp.sum(jnp.where(chosen, home_s[:, None, :], 0.0), axis=2)
+    return (
+        d_tok.astype(jnp.bfloat16),
+        d_probs,
+        grad_both[:, :part_width].astype(jnp.bfloat16)[None],
+        grad_both[:, part_width:].astype(jnp.bfloat16)[None],
+        grad_down.astype(jnp.bfloat16)[None],
+    )
+
+
+def gather_rows(block):
+    wide = lax.all_gather(block, "tp", axis=1, tiled=True)
+    return lax.all_gather(wide, ("role", "ep"), axis=0, tiled=True)
+
+
+def per_device(*arrays):
+    owners = lax.axis_size(("role", "ep"))
+    if owners <= 2 * arrays[2].shape[1]:
+        return dense_device(*arrays)
+    return routed_device(*arrays)
+
+
 def solution(mesh):
     in_specs = (
         P(("groups", "role", "ep"), "tp"),

time: 367 us -> 346 us (0.943)
  waiting for transfers between devices: 106 us -> 228 us
  blocking collectives: 148 us -> 34.4 us
  local copies, waits for them, and re-layouts: 37.4 us -> 6.77 us
  matrix products: 34.4 us -> 52.7 us
  other arithmetic: 20.2 us -> 5.46 us
    all_to_all x4 -> x1, blocking collectives: 143 us -> 8.93 us  [dense_device(): lax.all_to_all(send_p, ('role', 'ep'), split_axis=0, concat_axis=0, tiled...]
    all_gather x2, waiting for transfers between devices: 34.5 us -> 130 us  [gather_rows(): return lax.all_gather(wide, ('role', 'ep'), axis=0, tiled=True)]
    reduce_scatter x1 -> x2, waiting for transfers between devices: 43.3 us -> 92.4 us  [the longest x1 85.4 us: dense_device(): lax.psum_scatter(partial_low, ('role', 'ep'), scatter_dimension=0, tiled=...]
    gather x4 -> x0, local copies, waits for them, and re-layouts: 23.4 us -> none  [the longest x1 7.24 us: per_device(): send_prob = padded_prob[entry_of_slot].reshape(owners, capacity)]
    all_to_all x1, waiting for transfers between devices: 28 us -> 6.19 us  [dense_device(): lax.all_to_all(scores.reshape(owners, 1, tok_rows), ('role', 'ep'), split...]
    all_gather x0 -> x2, blocking collectives: none -> 20.5 us  [gather_rows(): wide = lax.all_gather(block, 'tp', axis=1, tiled=True)]
    dot_general x5, matrix products: 34.4 us -> 52.7 us  [the longest x1 12.2 us: dense_device(): lax.dot_general(rows_g, down_shard, (((1,), (1,)), ((), ())), preferred_e...]
    scatter-add x1 -> x0, other arithmetic: 14 us -> none  [per_device(): d_tok = jnp.zeros((tok_rows + 1, slice_width), jnp.float32).at[token_of_s...]
  transfers between devices with their start and end apart: 4 -> 5, of which waited for: 3 -> 5; matrix products, arithmetic and copies ran while one was open for 12% -> 11% of each run, Pallas kernels for 0% -> 0%
where the time goes in v1:
time: 346 us; the launch traced here: 345 us
  waiting for transfers between devices  228 us (66%)
  matrix products  52.7 us (15%)
  blocking collectives  34.4 us (10%)
  between operations  13.8 us (4%)
  local copies, waits for them, and re-layouts  6.77 us (2%)
  other arithmetic  5.46 us (2%)
  starting transfers between devices  3.82 us (1%)
    all_gather x2, waiting for transfers between devices, gather_rows(): return lax.all_gather(wide, ('role', 'ep'), axis=0, tiled=True)  130 us
    reduce_scatter x1, waiting for transfers between devices, dense_device(): lax.psum_scatter(partial_low, ('role', 'ep'), scatter_dimension=0, tiled=...  85.4 us
    all_gather x2, blocking collectives, gather_rows(): wide = lax.all_gather(block, 'tp', axis=1, tiled=True)  20.5 us
    dot_general x1, matrix products, dense_device(): lax.dot_general(rows_g, down_shard, (((1,), (1,)), ((), ())), preferred_e...  12.2 us
    dot_general x1, matrix products, dense_device(): both_rows = jnp.dot(rows_x, gate_up, preferred_element_type=jnp.float32)  11.8 us
    dot_general x1, matrix products, dense_device(): lax.dot_general(scaled, rows_g, (((0,), (0,)), ((), ())), preferred_eleme...  9.91 us
    dot_general x1, matrix products, dense_device(): lax.dot_general(rows_x, d_both, (((0,), (0,)), ((), ())), preferred_eleme...  9.65 us
    dot_general x1, matrix products, dense_device(): lax.dot_general(d_both, gate_up, (((1,), (1,)), ((), ())), preferred_elem...  9.12 us
  transfers between devices with their start and end apart: 5, of which 5 were waited for; matrix products, arithmetic and copies ran while one was open for 11% of the time, Pallas kernels for 0%

profile of v1, /device:TPU:0, one launch (start us, length us, event | category | flops | bytes accessed | tf_op | source)
XLA Modules:
  0.0 345.2 jit_solution(8791014049859605618)
XLA Ops:
  7.2 0.0 copy-start
  7.2 0.0 all-gather.5.cloned.1.call-start
  7.2 12.1 %all_gather.14 = bf16[128,2048]{1,0:T(8,128)(2,1)} all-gather(bf16[128,1024]{1,0:T(8,128)(2,1)} %param.7), channel_id=1, replica_groups=mesh['groups'=1,'role'=2,'ep'=8,'tp'=2] {'tp'}, dimensions={1}, use_global_device_ids=true | all-gather | bytes 786432 | tf_op jit(solution)/shard_map/all_gather | solution.py:174
  19.3 0.0 all-gather.5.cloned.1.call-update
  19.3 0.0 all-gather.3.cloned.1.call-start
  19.4 8.5 %all_gather.12 = bf16[128,2048]{1,0:T(8,128)(2,1)} all-gather(bf16[128,1024]{1,0:T(8,128)(2,1)} %param.8), channel_id=1, replica_groups=mesh['groups'=1,'role'=2,'ep'=8,'tp'=2] {'tp'}, dimensions={1}, use_global_device_ids=true | all-gather | bytes 786432 | tf_op jit(solution)/shard_map/all_gather | solution.py:174
  27.8 0.0 all-gather.3.cloned.1.call-update
  27.8 66.2 %all-gather.5.cloned.1.call-done = bf16[2048,2048]{1,0:T(8,128)(2,1)} async-done(((bf16[128,2048]{1,0:T(8,128)(2,1)}), bf16[2048,2048]{1,0:T(8,128)(2,1)}) %all-gather.5.cloned.1.call-update) | async-done | bytes 8388624 | tf_op jit(solution)/shard_map/all_gather | solution.py:175
  94.1 11.8 %convolution_bitcast_fusion = f32[2048,768]{0,1:T(8,128)} fusion(bf16[2048,2048]{1,0:T(8,128)(2,1)} %all-gather.5.cloned.1.call-done, bf16[2048,384]{1,0:T(8,128)(2,1)} %bitcast.37, bf16[2048,384]{1,0:T(8,128)(2,1)} %bitcast.39), kind=kOutput, calls=%fused_computation.1 | convolution fusion | flops 6448742400 | bytes 17825792 | tf_op jit(solution)/shard_map/dot_general | solution.py:131
  105.9 0.0 copy-start.3
  105.9 0.0 copy-start.2
  105.9 63.3 %all-gather.3.cloned.1.call-done = bf16[2048,2048]{1,0:T(8,128)(2,1)} async-done(((bf16[128,2048]{1,0:T(8,128)(2,1)}), bf16[2048,2048]{1,0:T(8,128)(2,1)}) %all-gather.3.cloned.1.call-update) | async-done | bytes 8388624 | tf_op jit(solution)/shard_map/all_gather | solution.py:175
  169.2 0.0 copy-done
  169.2 12.2 %multiply_reduce_fusion = (f32[2048]{0:T(1024)}, f32[2048,384]{0,1:T(8,128)}) fusion(f32[2048,768]{0,1:T(8,128)} %convolution_bitcast_fusion, bf16[2048,2048]{1,0:T(8,128)(2,1)} %all-gather.3.cloned.1.call-done, bf16[1,384,2048]{2,1,0:T(8,128)(2,1)S(1)} %copy-done), kind=kOutput, calls=%fused_computation.6 | convolution fusion | flops 3226728448 | bytes 19406848 | tf_op jit(solution)/shard_map/dot_general | solution.py:137
  181.4 3.5 %all-to-all-start.1 = ((f32[16,1,128]{2,1,0:T(1,128)}), f32[16,1,128]{2,1,0:T(1,128)S(1)}, u32[]{:S(2)}, u32[]{:S(2)}) async-start(f32[16,1,128]{2,1,0:T(1,128)} %bitcast.8), calls=%async_computation.3 | async-start | bytes 16384 | tf_op jit(solution)/shard_map/all_to_all | solution.py:159
  184.9 0.0 reduce-scatter.3.cloned.1.call-start
  185.0 0.0 copy-done.3
  185.0 6.2 %all-to-all-done.1 = f32[16,1,128]{2,1,0:T(1,128)S(1)} async-done(((f32[16,1,128]{2,1,0:T(1,128)}), f32[16,1,128]{2,1,0:T(1,128)S(1)}, u32[]{:S(2)}, u32[]{:S(2)}) %all-to-all-start.1) | async-done | bytes 8224 | tf_op jit(solution)/shard_map/all_to_all | solution.py:159
  191.2 5.0 %psum.7 = f32[128,16]{0,1:T(8,128)S(1)} all-reduce(f32[128,16]{0,1:T(8,128)S(1)} %bitcast.35), channel_id=1, replica_groups=mesh['groups'=1,'role'=2,'ep'=8,'tp'=2] {'tp'}, use_global_device_ids=true, to_apply=%region_4.5 | all-reduce | flops 2048 | bytes 16384 | tf_op jit(solution)/shard_map/psum | solution.py:162
  196.1 0.0 copy-done.2
  196.1 0.6 select_reduce_fusion
  196.8 8.9 %all_to_all.10 = bf16[16,1,128]{2,1,0:T(2,128)(2,1)S(1)} all-to-all(bf16[16,1,128]{2,1,0:T(2,128)(2,1)S(1)} %copy.36), channel_id=1, replica_groups=mesh['groups'=1,'role'=2,'ep'=8,'tp'=2] {'role','ep'}, dimensions={0} | all-to-all | bytes 8192 | tf_op jit(solution)/shard_map/all_to_all | solution.py:125
  205.7 0.0 copy-start.4
  205.7 0.0 copy-start.5
  205.7 4.8 %multiply_convert_fusion.2 = (bf16[2048,384]{0,1:T(8,128)(2,1)S(1)}, bf16[2048,384]{0,1:T(8,128)(2,1)S(1)}) fusion(f32[2048,768]{0,1:T(8,128)} %convolution_bitcast_fusion, f32[2048,384]{0,1:T(8,128)} %get-tuple-element.37, f32[2048]{0:T(1024)S(1)} %bitcast_convert_fusion), kind=kLoop, calls=%fused_computation.8 | loop fusion | flops 11010048 | bytes 12591104 | tf_op jit(solution)/shard_map/convert_element_type | solution.py:144
  210.5 0.0 copy-start.1
  210.6 1.1 copy-done.1
  211.7 0.0 copy-done.4
  211.7 0.0 copy-done.5
  211.7 9.1 %convolution_convert_fusion = bf16[2048,2048]{1,0:T(8,128)(2,1)} fusion(bf16[2048,384]{0,1:T(8,128)(2,1)S(1)} %get-tuple-element.33, bf16[2048,384]{0,1:T(8,128)(2,1)S(1)} %get-tuple-element.32, bf16[2048,384]{1,0:T(8,128)(2,1)S(1)} %bitcast.38, bf16[2048,384]{1,0:T(8,128)(2,1)S(1)} %bitcast.40), kind=kOutput, calls=%fused_computation | convolution fusion | flops 6459228160 | bytes 14680064 | tf_op jit(solution)/shard_map/dot_general | solution.py:148
  220.8 0.0 reduce-scatter.3.cloned.1.call-update
  220.8 0.2 reduce-scatter.5.cloned.1.call-start
  221.1 9.6 %fusion.1 = bf16[2048,768]{0,1:T(8,128)(2,1)S(1)} fusion(bf16[2048,2048]{1,0:T(8,128)(2,1)} %all-gather.5.cloned.1.call-done, bf16[2048,384]{0,1:T(8,128)(2,1)} %copy-done.1, bf16[2048,384]{0,1:T(8,128)(2,1)S(1)} %get-tuple-element.32), kind=kOutput, calls=%fused_computation.11 | convolution fusion | flops 6450315264 | bytes 14680064 | tf_op jit(solution)/shard_map/dot_general | solution.py:156
  230.7 1.4 slice_bitcast_fusion
  232.1 2.7 copy.40
  234.8 1.6 copy.39
  236.3 85.4 %reduce-scatter.3.cloned.1.call-done = bf16[128,2048]{1,0:T(8,128)(2,1)} async-done(((bf16[2048,2048]{1,0:T(8,128)(2,1)}), bf16[128,2048]{1,0:T(8,128)(2,1)}) %reduce-scatter.3.cloned.1.call-update) | async-done | bytes 524304 | tf_op jit(solution)/shard_map/reduce_scatter | solution.py:151
  321.7 0.0 reduce-scatter.5.cloned.1.call-update
  321.7 9.9 %fusion.2 = bf16[1,384,2048]{2,1,0:T(8,128)(2,1)} fusion(bf16[2048,2048]{1,0:T(8,128)(2,1)} %all-gather.3.cloned.1.call-done, f32[2048]{0:T(1024)S(1)} %bitcast_convert_fusion, f32[2048,768]{0,1:T(8,128)} %convolution_bitcast_fusion), kind=kOutput, calls=%fused_computation.14 | convolution fusion | flops 3227516928 | bytes 16261120 | tf_op jit(solution)/shard_map/dot_general | solution.py:153
  331.6 7.0 %reduce-scatter.5.cloned.1.call-done = bf16[128,1024]{1,0:T(8,128)(2,1)} async-done(((bf16[128,2048]{1,0:T(8,128)(2,1)}), bf16[128,1024]{1,0:T(8,128)(2,1)}) %reduce-scatter.5.cloned.1.call-update) | async-done | bytes 262160 | tf_op jit(solution)/shard_map/reduce_scatter | solution.py:152
  (3 shorter events, 0.0 us)
Async XLA Ops:
  7.2 162.0 %copy-start = (bf16[1,384,2048]{2,1,0:T(8,128)(2,1)S(1)}, bf16[1,384,2048]{2,1,0:T(8,128)(2,1)}, u32[]{:S(2)}) copy-start(bf16[1,384,2048]{2,1,0:T(8,128)(2,1)} %param.13) | copy-start | bytes 4718596
  7.2 86.9 %all-gather.5.cloned.1.call-start = ((), (), s32[]{:S(2)}) async-start(), calls=%async_computation.5 | async-start | bytes 8912896 | tf_op jit(solution)/shard_map/all_gather | solution.py:175
  19.3 149.9 %all-gather.3.cloned.1.call-start = ((), (), s32[]{:S(2)}) async-start(), calls=%async_computation.4 | async-start | bytes 8912896 | tf_op jit(solution)/shard_map/all_gather | solution.py:175
  105.9 79.1 %copy-start.3 = (bf16[128,8]{0,1:T(8,128)(2,1)S(1)}, bf16[128,8]{0,1:T(8,128)(2,1)}, u32[]{:S(2)}) copy-start(bf16[128,8]{0,1:T(8,128)(2,1)} %param.10) | copy-start | bytes 6148
  105.9 90.2 %copy-start.2 = (s32[128,8]{0,1:T(8,128)S(1)}, s32[128,8]{0,1:T(8,128)}, u32[]{:S(2)}) copy-start(s32[128,8]{0,1:T(8,128)} %param.9) | copy-start | bytes 12292
  181.4 9.7 %all-to-all-start.1 = ((f32[16,1,128]{2,1,0:T(1,128)}), f32[16,1,128]{2,1,0:T(1,128)S(1)}, u32[]{:S(2)}, u32[]{:S(2)}) async-start(f32[16,1,128]{2,1,0:T(1,128)} %bitcast.8), calls=%async_computation.3 | async-start | bytes 16384 | tf_op jit(solution)/shard_map/all_to_all | solution.py:159
  184.9 136.8 %reduce-scatter.3.cloned.1.call-start = ((), (), s32[]{:S(2)}) async-start(), calls=%async_computation.6 | async-start | bytes 8912896 | tf_op jit(solution)/shard_map/reduce_scatter | solution.py:151
  205.7 6.0 %copy-start.4 = (bf16[1,2048,384]{2,1,0:T(8,128)(2,1)S(1)}, bf16[1,2048,384]{2,1,0:T(8,128)(2,1)}, u32[]{:S(2)}) copy-start(bf16[1,2048,384]{2,1,0:T(8,128)(2,1)} %param.12) | copy-start | bytes 4718596
  205.7 6.0 %copy-start.5 = (bf16[1,2048,384]{2,1,0:T(8,128)(2,1)S(1)}, bf16[1,2048,384]{2,1,0:T(8,128)(2,1)}, u32[]{:S(2)}) copy-start(bf16[1,2048,384]{2,1,0:T(8,128)(2,1)} %param.11) | copy-start | bytes 4718596
  210.5 1.1 copy-start.1
  220.8 117.8 %reduce-scatter.5.cloned.1.call-start = ((), (), s32[]{:S(2)}) async-start(), calls=%async_computation.7 | async-start | bytes 786432 | tf_op jit(solution)/shard_map/reduce_scatter | solution.py:152
Sparse Core Ops, SparseCore 0:
  19.4 74.6 all-gather.4
  96.3 72.8 all-gather.2
  221.0 100.6 reduce-scatter.2
  324.4 14.2 reduce-scatter.4

commit v2 on v1

--- a/solution.py
+++ b/solution.py
@@ -112,22 +112,24 @@
     )
 
 
-def dense_device(tokens, out_grad, routes, probs, w_gate, w_up, w_down):
-    owners = lax.axis_size(("role", "ep"))
-    tok_rows, top_count = routes.shape
-    part_width = w_gate.shape[2]
-    experts = jnp.arange(owners, dtype=jnp.int32)
-    chosen = routes[:, :, None] == experts[None, None, :]
-    prob_table = jnp.sum(
-        jnp.where(chosen, probs[:, :, None].astype(jnp.float32), 0.0), axis=1
-    )
-    send_p = prob_table.T.astype(jnp.bfloat16).reshape(owners, 1, tok_rows)
-    recv_p = lax.all_to_all(send_p, ("role", "ep"), split_axis=0, concat_axis=0, tiled=True)
-    weight_p = recv_p.reshape(owners * tok_rows, 1).astype(jnp.float32)
-    rows_x = gather_rows(tokens)
-    rows_g = gather_rows(out_grad)
-    gate_up = jnp.concatenate([w_gate[0], w_up[0]], 1)
-    down_shard = w_down[0]
+def swap(block, axis):
+    return lax.ppermute(block, axis, ((0, 1), (1, 0)))
+
+
+def own_first(pair):
+    return jnp.where(lax.axis_index("role") == 0, pair, pair[::-1])
+
+
+def widen(block):
+    other = swap(block, "tp")
+    first = lax.axis_index("tp") == 0
+    low = jnp.where(first, block, other)
+    high = jnp.where(first, other, block)
+    return jnp.concatenate([low, high], 1)
+
+
+def half_rows(rows_x, rows_g, weight_p, gate_up, down_shard):
+    part_width = down_shard.shape[0]
     both_rows = jnp.dot(rows_x, gate_up, preferred_element_type=jnp.float32)
     gate_rows = both_rows[:, :part_width]
     up_rows = both_rows[:, part_width:]
@@ -148,18 +150,60 @@
     partial_low = lax.dot_general(
         d_both, gate_up, (((1,), (1,)), ((), ())), preferred_element_type=jnp.float32
     ).astype(jnp.bfloat16)
-    summed = lax.psum_scatter(partial_low, ("role", "ep"), scatter_dimension=0, tiled=True)
-    d_tok = lax.psum_scatter(summed, "tp", scatter_dimension=1, tiled=True)
-    grad_down = lax.dot_general(
-        scaled, rows_g, (((0,), (0,)), ((), ())), preferred_element_type=jnp.float32
-    )
-    grad_both = lax.dot_general(
-        rows_x, d_both, (((0,), (0,)), ((), ())), preferred_element_type=jnp.float32
-    )
+    return scores, d_both, scaled, partial_low
+
+
+def row_dot(left, right):
+    return lax.dot_general(
+        left, right, (((0,), (0,)), ((), ())), preferred_element_type=jnp.float32
+    )
+
+
+def dense_device(tokens, out_grad, routes, probs, w_gate, w_up, w_down):
+    owners = lax.axis_size(("role", "ep"))
+    tok_rows, top_count = routes.shape
+    half_count = owners * tok_rows // 2
+    slice_width = tokens.shape[1]
+    part_width = w_gate.shape[2]
+    experts = jnp.arange(owners, dtype=jnp.int32)
+    chosen = routes[:, :, None] == experts[None, None, :]
+    prob_table = jnp.sum(
+        jnp.where(chosen, probs[:, :, None].astype(jnp.float32), 0.0), axis=1
+    )
+    own_x = lax.all_gather(widen(tokens), "ep", axis=0, tiled=True)
+    send_p = prob_table.T.astype(jnp.bfloat16).reshape(owners, 1, tok_rows)
+    recv_p = lax.all_to_all(send_p, ("role", "ep"), split_axis=0, concat_axis=0, tiled=True)
+    recv_p, out_grad = lax.optimization_barrier((recv_p, out_grad))
+    weight_p = own_first(recv_p.reshape(2, half_count)).astype(jnp.float32)
+    own_g = lax.all_gather(widen(out_grad), "ep", axis=0, tiled=True)
+    other_x = swap(own_x, "role")
+    other_g = swap(own_g, "role")
+    gate_up = jnp.concatenate([w_gate[0], w_up[0]], 1)
+    down_shard = w_down[0]
+    other_s, other_d, other_scaled, other_low = half_rows(
+        other_x, other_g, weight_p[1][:, None], gate_up, down_shard
+    )
+    own_s, own_d, own_scaled, own_low = half_rows(
+        own_x, own_g, weight_p[0][:, None], gate_up, down_shard
+    )
+    crossed = swap(other_low, "role")
+    joined = (own_low.astype(jnp.float32) + crossed.astype(jnp.float32)).astype(jnp.bfloat16)
+    scores, joined = lax.optimization_barrier((jnp.stack([own_s, other_s]), joined))
+    summed = lax.psum_scatter(joined, "ep", scatter_dimension=0, tiled=True)
+    first = lax.axis_index("tp") == 0
+    low, high = summed[:, :slice_width], summed[:, slice_width:]
+    kept = jnp.where(first, low, high).astype(jnp.float32)
+    d_tok = kept + swap(jnp.where(first, high, low), "tp").astype(jnp.float32)
+    grad_down = row_dot(own_scaled, own_g) + row_dot(other_scaled, other_g)
+    grad_both = row_dot(own_x, own_d) + row_dot(other_x, other_d)
     home_s = lax.all_to_all(
-        scores.reshape(owners, 1, tok_rows), ("role", "ep"), split_axis=0, concat_axis=0, tiled=True
-    )
-    home_s = lax.psum(home_s, "tp").reshape(owners, tok_rows).T
+        own_first(scores).reshape(owners, 1, tok_rows),
+        ("role", "ep"),
+        split_axis=0,
+        concat_axis=0,
+        tiled=True,
+    )
+    home_s = (home_s + swap(home_s, "tp")).reshape(owners, tok_rows).T
     d_probs = jnp.sum(jnp.where(chosen, home_s[:, None, :], 0.0), axis=2)
     return (
         d_tok.astype(jnp.bfloat16),
@@ -170,14 +214,10 @@
     )
 
 
-def gather_rows(block):
-    wide = lax.all_gather(block, "tp", axis=1, tiled=True)
-    return lax.all_gather(wide, ("role", "ep"), axis=0, tiled=True)
-
-
 def per_device(*arrays):
     owners = lax.axis_size(("role", "ep"))
-    if owners <= 2 * arrays[2].shape[1]:
+    pairs = lax.axis_size("role") == 2 and lax.axis_size("tp") == 2
+    if pairs and owners <= 2 * arrays[2].shape[1]:
         return dense_device(*arrays)
     return routed_device(*arrays)
 

time: 346 us -> 314 us (0.908)
  blocking collectives: 34.4 us -> 0 us
  starting transfers between devices: 3.82 us -> 17.7 us
  waiting for transfers between devices: 228 us -> 219 us
    reduce_scatter x2 -> x1, waiting for transfers between devices: 92.4 us -> 56.7 us  [dense_device(): summed = lax.psum_scatter(joined, 'ep', scatter_dimension=0, tiled=True)]
    all_gather x2 -> x0, blocking collectives: 20.5 us -> none  [gather_rows(): wide = lax.all_gather(block, 'tp', axis=1, tiled=True)]
    all_gather x2, waiting for transfers between devices: 130 us -> 147 us  [the longest x1 74.1 us: dense_device(): own_g = lax.all_gather(widen(out_grad), 'ep', axis=0, tiled=True)]
    ppermute x0 -> x7, waiting for transfers between devices: none -> 9.97 us  [swap(): return lax.ppermute(block, axis, ((0, 1), (1, 0)))]
    all_to_all x1 -> x0, blocking collectives: 8.93 us -> none  [dense_device(): lax.all_to_all(send_p, ('role', 'ep'), split_axis=0, concat_axis=0, tiled...]
    all_to_all x1 -> x2, starting transfers between devices: 3.47 us -> 10.9 us  [the longest x1 7.41 us: dense_device(): lax.all_to_all(send_p, ('role', 'ep'), split_axis=0, concat_axis=0, tiled...]
    ppermute x0 -> x7, starting transfers between devices: none -> 6.66 us  [swap(): return lax.ppermute(block, axis, ((0, 1), (1, 0)))]
    unnamed x14 -> x28, local copies, waits for them, and re-layouts: 5.4 us -> 0.07 us
  transfers between devices with their start and end apart: 5 -> 12, of which waited for: 5 -> 9; matrix products, arithmetic and copies ran while one was open for 11% -> 14% of each run, Pallas kernels for 0% -> 0%
where the time goes in v2:
time: 314 us; the launch traced here: 313 us
  waiting for transfers between devices  219 us (70%)
  matrix products  50.7 us (16%)
  starting transfers between devices  17.7 us (6%)
  between operations  14.1 us (4%)
  other arithmetic  6.84 us (2%)
  local copies, waits for them, and re-layouts  5.59 us (2%)
    all_gather x1, waiting for transfers between devices, dense_device(): own_g = lax.all_gather(widen(out_grad), 'ep', axis=0, tiled=True)  74.1 us
    all_gather x1, waiting for transfers between devices, dense_device(): own_x = lax.all_gather(widen(tokens), 'ep', axis=0, tiled=True)  73 us
    reduce_scatter x1, waiting for transfers between devices, dense_device(): summed = lax.psum_scatter(joined, 'ep', scatter_dimension=0, tiled=True)  56.7 us
    dot_general x4, matrix products, row_dot(): lax.dot_general(left, right, (((0,), (0,)), ((), ())), preferred_element_...  24.6 us
    ppermute x7, waiting for transfers between devices, swap(): return lax.ppermute(block, axis, ((0, 1), (1, 0)))  9.97 us
    dot_general x2, matrix products, half_rows(): both_rows = jnp.dot(rows_x, gate_up, preferred_element_type=jnp.float32)  9.83 us
    dot_general x2, matrix products, half_rows(): lax.dot_general(d_both, gate_up, (((1,), (1,)), ((), ())), preferred_elem...  8.88 us
    all_to_all x1, starting transfers between devices, dense_device(): lax.all_to_all(send_p, ('role', 'ep'), split_axis=0, concat_axis=0, tiled...  7.41 us
  transfers between devices with their start and end apart: 12, of which 9 were waited for; matrix products, arithmetic and copies ran while one was open for 14% of the time, Pallas kernels for 0%

profile of v2, /device:TPU:0, one launch (start us, length us, event | category | flops | bytes accessed | tf_op | source)
XLA Modules:
  0.0 313.4 jit_solution(1950335930562845120)
XLA Ops:
  7.2 0.0 copy-start
  7.2 0.8 convert_element_type.60
  8.0 0.7 select_reduce_fusion.1
  8.7 0.6 copy.26
  9.3 7.4 %all-to-all-start = ((bf16[16,1,128]{2,1,0:T(2,128)(2,1)}), bf16[16,1,128]{2,1,0:T(2,128)(2,1)S(1)}, u32[]{:S(2)}, u32[]{:S(2)}) async-start(bf16[16,1,128]{2,1,0:T(2,128)(2,1)} %copy.26), calls=%async_computation | async-start | bytes 16384 | tf_op jit(solution)/shard_map/all_to_all | solution.py:175
  16.7 0.0 all-gather.3.cloned.1.call-start
  16.8 1.6 collective-permute-start
  18.3 4.7 %all-to-all-done = bf16[16,1,128]{2,1,0:T(2,128)(2,1)S(1)} async-done(((bf16[16,1,128]{2,1,0:T(2,128)(2,1)}), bf16[16,1,128]{2,1,0:T(2,128)(2,1)S(1)}, u32[]{:S(2)}, u32[]{:S(2)}) %all-to-all-start) | async-done | bytes 4128 | tf_op jit(solution)/shard_map/all_to_all | solution.py:175
  23.1 1.5 collective-permute-start.1
  24.5 1.1 collective-permute-done
  25.7 5.6 %collective-permute-done.1 = bf16[128,1024]{1,0:T(8,128)(2,1)S(1)} collective-permute-done((bf16[128,1024]{1,0:T(8,128)(2,1)}, bf16[128,1024]{1,0:T(8,128)(2,1)S(1)}, u32[]{:S(2)}, u32[]{:S(2)}) %collective-permute-start.1) | collective-permute-done | bytes 262176 | tf_op jit(solution)/shard_map/ppermute | solution.py:116
  31.3 1.1 broadcast_select_fusion.2
  32.4 0.8 pad_maximum_fusion.7
  33.2 0.0 all-gather.3.cloned.1.call-update
  33.2 0.0 all-gather.5.cloned.1.call-start
  33.3 0.8 pad_maximum_fusion.8
  34.1 0.0 all-gather.5.cloned.1.call-update
  34.1 0.0 reduce-scatter.2.cloned.1.call-start
  34.2 73.0 %all-gather.3.cloned.1.call-done = bf16[1024,2048]{1,0:T(8,128)(2,1)} async-done(((bf16[128,2048]{1,0:T(8,128)(2,1)}), bf16[1024,2048]{1,0:T(8,128)(2,1)}) %all-gather.3.cloned.1.call-update) | async-done | bytes 4194320 | tf_op jit(solution)/shard_map/all_gather | solution.py:173
  107.2 0.0 collective-permute-start.2
  107.2 74.1 %all-gather.5.cloned.1.call-done = bf16[1024,2048]{1,0:T(8,128)(2,1)} async-done(((bf16[128,2048]{1,0:T(8,128)(2,1)}), bf16[1024,2048]{1,0:T(8,128)(2,1)}) %all-gather.5.cloned.1.call-update) | async-done | bytes 4194320 | tf_op jit(solution)/shard_map/all_gather | solution.py:178
  181.3 0.0 collective-permute-start.3
  181.3 0.2 rev.6
  181.6 0.0 collective-permute-done.2
  181.6 6.2 %fusion.16 = f32[1024,768]{0,1:T(8,128)S(1)} fusion(bf16[1024,2048]{1,0:T(8,128)(2,1)} %collective-permute-done.2, bf16[2048,384]{1,0:T(8,128)(2,1)} %bitcast.46, bf16[2048,384]{1,0:T(8,128)(2,1)} %bitcast.50), kind=kOutput, calls=%fused_computation.52 | convolution fusion | flops 3227516928 | bytes 10485760 | tf_op jit(solution)/shard_map/dot_general | solution.py:133
  187.8 0.0 copy-start.9
  187.8 0.9 collective-permute-done.3
  188.8 4.9 %multiply_convert_fusion.3 = (bf16[1024,384]{0,1:T(8,128)(2,1)S(1)}, bf16[1024,384]{0,1:T(8,128)(2,1)S(1)}, f32[1024]{0:T(1024)S(1)}) fusion(f32[1024,768]{0,1:T(8,128)S(1)} %fusion.16, f32[1024]{0:T(1024)S(1)} %bitcast.42, bf16[1024,2048]{1,0:T(8,128)(2,1)} %collective-permute-done.3, bf16[1,384,2048]{2,1,0:T(8,128)(2,1)S(1)} %copy-done), kind=kOutput, calls=%fused_computation.17 | convolution fusion | flops 1617296384 | bytes 10493952 | tf_op jit(solution)/shard_map/dot_general | solution.py:139
  193.6 0.0 copy-start.10
  193.6 0.0 copy-start.12
  193.7 0.0 copy-done.6
  193.7 0.0 copy-done.7
  193.7 0.0 copy-start.4
  193.7 3.7 %convolution_convert_fusion = bf16[1024,2048]{1,0:T(8,128)(2,1)S(1)} fusion(bf16[1024,384]{0,1:T(8,128)(2,1)S(1)} %get-tuple-element.16, bf16[1024,384]{0,1:T(8,128)(2,1)S(1)} %get-tuple-element.15, bf16[2048,384]{1,0:T(8,128)(2,1)S(1)} %bitcast.47, bf16[2048,384]{1,0:T(8,128)(2,1)S(1)} %bitcast.51), kind=kOutput, calls=%fused_computation.2 | convolution fusion | flops 3232759808 | bytes 8912896 | tf_op jit(solution)/shard_map/dot_general | solution.py:150
  197.5 0.6 collective-permute-start.4
  198.1 3.6 %fusion.17 = f32[1024,768]{0,1:T(8,128)S(1)} fusion(bf16[1024,2048]{1,0:T(8,128)(2,1)S(1)} %copy-done.4, bf16[2048,384]{1,0:T(8,128)(2,1)S(1)} %bitcast.48, bf16[2048,384]{1,0:T(8,128)(2,1)S(1)} %bitcast.52), kind=kOutput, calls=%fused_computation.53 | convolution fusion | flops 3227516928 | bytes 10485760 | tf_op jit(solution)/shard_map/dot_general | solution.py:133
  201.7 0.0 copy-start.8
  201.7 0.0 copy-done.3
  201.7 2.5 multiply_convert_fusion.5
  204.2 0.6 collective-permute-done.4
  204.8 5.2 %add_convert_fusion = bf16[1024,2048]{1,0:T(8,128)(2,1)} fusion(bf16[1024,2048]{1,0:T(8,128)(2,1)S(1)} %collective-permute-done.4, bf16[1024,384]{0,1:T(8,128)(2,1)S(1)} %get-tuple-element.14, bf16[1024,384]{0,1:T(8,128)(2,1)S(1)} %get-tuple-element.13, bf16[2048,384]{1,0:T(8,128)(2,1)S(1)} %bitcast.49, bf16[2048,384]{1,0:T(8,128)(2,1)S(1)} %bitcast.53), kind=kOutput, calls=%fused_computation | convolution fusion | flops 3241148416 | bytes 13107200 | tf_op jit(solution)/shard_map/dot_general | solution.py:150
  210.0 0.0 reduce-scatter.2.cloned.1.call-update
  210.0 0.0 copy-start.11
  210.0 0.0 copy-start.13
  210.1 6.9 %fusion.8 = f32[384,2048]{1,0:T(8,128)} fusion(bf16[1024,2048]{1,0:T(8,128)(2,1)} %collective-permute-done.3, f32[1024]{0:T(1024)S(1)} %bitcast.43, f32[1024,768]{0,1:T(8,128)} %copy-done.9), kind=kOutput, calls=%fused_computation.29 | convolution fusion | flops 1613365248 | bytes 10489856 | tf_op jit(solution)/shard_map/dot_general | solution.py:157
  216.9 5.5 %fusion.7 = f32[2048,768]{1,0:T(8,128)S(1)} fusion(bf16[1024,2048]{1,0:T(8,128)(2,1)} %collective-permute-done.2, bf16[1024,384]{0,1:T(8,128)(2,1)S(1)} %copy-done.13, bf16[1024,384]{0,1:T(8,128)(2,1)S(1)} %copy-done.11), kind=kOutput, calls=%fused_computation.28 | convolution fusion | flops 3224371200 | bytes 12058624 | tf_op jit(solution)/shard_map/dot_general | solution.py:157
  222.4 0.0 copy-done.5
  222.4 5.0 %add_convert_fusion.1 = bf16[2048,768]{1,0:T(8,128)(2,1)} fusion(f32[2048,768]{1,0:T(8,128)S(1)} %fusion.7, bf16[1024,2048]{1,0:T(8,128)(2,1)S(1)} %copy-done.5, bf16[1024,384]{0,1:T(8,128)(2,1)S(1)} %get-tuple-element.14, bf16[1024,384]{0,1:T(8,128)(2,1)S(1)} %get-tuple-element.13), kind=kOutput, calls=%fused_computation.1 | convolution fusion | flops 3227516928 | bytes 15204352 | tf_op jit(solution)/shard_map/dot_general | solution.py:157
  227.4 0.2 rev.7
  227.6 0.6 reshape.30
  228.2 3.5 %all-to-all-start.1 = ((f32[16,1,128]{2,1,0:T(1,128)}), f32[16,1,128]{2,1,0:T(1,128)S(1)}, u32[]{:S(2)}, u32[]{:S(2)}) async-start(f32[16,1,128]{2,1,0:T(1,128)} %bitcast.9), calls=%async_computation.2 | async-start | bytes 16384 | tf_op jit(solution)/shard_map/all_to_all | solution.py:199
  231.7 7.3 %fusion = bf16[1,384,2048]{2,1,0:T(8,128)(2,1)} fusion(f32[384,2048]{1,0:T(8,128)} %fusion.8, bf16[1024,2048]{1,0:T(8,128)(2,1)} %all-gather.5.cloned.1.call-done, f32[1024]{0:T(1024)S(1)} %bitcast.41, f32[1024,768]{0,1:T(8,128)} %copy-done.8), kind=kOutput, calls=%fused_computation.5 | convolution fusion | flops 1614938112 | bytes 12062720 | tf_op jit(solution)/shard_map/dot_general | solution.py:157
  239.0 0.0 all-to-all-done.1
  239.0 1.5 collective-permute-start.6
  240.5 56.7 %reduce-scatter.2.cloned.1.call-done = bf16[128,2048]{1,0:T(8,128)(2,1)} async-done(((bf16[1024,2048]{1,0:T(8,128)(2,1)}), bf16[128,2048]{1,0:T(8,128)(2,1)}) %reduce-scatter.2.cloned.1.call-update) | async-done | bytes 524304 | tf_op jit(solution)/shard_map/reduce_scatter | solution.py:192
  297.2 1.1 broadcast_select_fusion
  298.3 0.0 copy-start.2
  298.3 1.5 collective-permute-start.5
  299.8 3.9 %slice_bitcast_fusion = (bf16[1,2048,384]{2,1,0:T(8,128)(2,1)}, bf16[1,2048,384]{2,1,0:T(8,128)(2,1)}) fusion(bf16[2048,768]{1,0:T(8,128)(2,1)} %add_convert_fusion.1), kind=kLoop, calls=%fused_computation.6 | loop fusion | bytes 6291456 | tf_op jit(solution)/shard_map/broadcast_in_dim | solution.py:212
  303.7 0.0 collective-permute-done.6
  303.7 0.6 select_reduce_fusion
  304.3 1.7 collective-permute-done.5
  306.0 0.0 copy-done.1
  306.0 0.8 add_convert_fusion.3
  (21 shorter events, 0.1 us)
Async XLA Ops:
  7.2 181.6 %copy-start = (bf16[1,384,2048]{2,1,0:T(8,128)(2,1)S(1)}, bf16[1,384,2048]{2,1,0:T(8,128)(2,1)}, u32[]{:S(2)}) copy-start(bf16[1,384,2048]{2,1,0:T(8,128)(2,1)} %param.13) | copy-start | bytes 4718596
  9.3 13.8 %all-to-all-start = ((bf16[16,1,128]{2,1,0:T(2,128)(2,1)}), bf16[16,1,128]{2,1,0:T(2,128)(2,1)S(1)}, u32[]{:S(2)}, u32[]{:S(2)}) async-start(bf16[16,1,128]{2,1,0:T(2,128)(2,1)} %copy.26), calls=%async_computation | async-start | bytes 16384 | tf_op jit(solution)/shard_map/all_to_all | solution.py:175
  16.7 90.5 %all-gather.3.cloned.1.call-start = ((), (), s32[]{:S(2)}) async-start(), calls=%async_computation.3 | async-start | bytes 4718592 | tf_op jit(solution)/shard_map/all_gather | solution.py:173
  16.8 8.9 %collective-permute-start = (bf16[128,1024]{1,0:T(8,128)(2,1)}, bf16[128,1024]{1,0:T(8,128)(2,1)S(1)}, u32[]{:S(2)}, u32[]{:S(2)}) collective-permute-start(bf16[128,1024]{1,0:T(8,128)(2,1)} %param.7), channel_id=1, source_target_pairs={{0,1},{1,0},{2,3},{3,2},{4,5},{5,4},{6,7},{7,6},{8,9},{9,8},{10,11... | collective-permute-start | bytes 786440 | tf_op jit(solution)/shard_map/ppermute | solution.py:116
  23.1 8.2 %collective-permute-start.1 = (bf16[128,1024]{1,0:T(8,128)(2,1)}, bf16[128,1024]{1,0:T(8,128)(2,1)S(1)}, u32[]{:S(2)}, u32[]{:S(2)}) collective-permute-start(bf16[128,1024]{1,0:T(8,128)(2,1)} %param.8), channel_id=1, source_target_pairs={{0,1},{1,0},{2,3},{3,2},{4,5},{5,4},{6,7},{7,6},{8,9},{9,8},{10,11... | collective-permute-start | bytes 786440 | tf_op jit(solution)/shard_map/ppermute | solution.py:116
  33.2 148.0 %all-gather.5.cloned.1.call-start = ((), (), s32[]{:S(2)}) async-start(), calls=%async_computation.4 | async-start | bytes 4718592 | tf_op jit(solution)/shard_map/all_gather | solution.py:178
  34.1 263.1 %reduce-scatter.2.cloned.1.call-start = ((), (), s32[]{:S(2)}) async-start(), calls=%async_computation.5 | async-start | bytes 4718592 | tf_op jit(solution)/shard_map/reduce_scatter | solution.py:192
  107.2 74.4 %collective-permute-start.2 = (bf16[1024,2048]{1,0:T(8,128)(2,1)}, bf16[1024,2048]{1,0:T(8,128)(2,1)}, u32[]{:S(2)}, u32[]{:S(2)}) collective-permute-start(bf16[1024,2048]{1,0:T(8,128)(2,1)} %all-gather.3.cloned.1.call-done), channel_id=1, source_target_pairs={{0,16},{16,0},{1,17},{17,1},{2,18},{18,2},{3,19},{19,3},{4,20},{20... | collective-permute-start | bytes 12582920 | tf_op jit(solution)/shard_map/ppermute | solution.py:116
  181.3 7.5 %collective-permute-start.3 = (bf16[1024,2048]{1,0:T(8,128)(2,1)}, bf16[1024,2048]{1,0:T(8,128)(2,1)}, u32[]{:S(2)}, u32[]{:S(2)}) collective-permute-start(bf16[1024,2048]{1,0:T(8,128)(2,1)} %all-gather.5.cloned.1.call-done), channel_id=1, source_target_pairs={{0,16},{16,0},{1,17},{17,1},{2,18},{18,2},{3,19},{19,3},{4,20},{20... | collective-permute-start | bytes 12582920 | tf_op jit(solution)/shard_map/ppermute | solution.py:116
  187.8 5.8 %copy-start.9 = (f32[1024,768]{0,1:T(8,128)}, f32[1024,768]{0,1:T(8,128)S(1)}, u32[]{:S(2)}) copy-start(f32[1024,768]{0,1:T(8,128)S(1)} %fusion.16) | copy-start | bytes 9437188
  188.8 4.9 %copy-start.6 = (bf16[1,2048,384]{2,1,0:T(8,128)(2,1)S(1)}, bf16[1,2048,384]{2,1,0:T(8,128)(2,1)}, u32[]{:S(2)}) copy-start(bf16[1,2048,384]{2,1,0:T(8,128)(2,1)} %param.12) | copy-start | bytes 4718596
  188.8 4.9 %copy-start.7 = (bf16[1,2048,384]{2,1,0:T(8,128)(2,1)S(1)}, bf16[1,2048,384]{2,1,0:T(8,128)(2,1)}, u32[]{:S(2)}) copy-start(bf16[1,2048,384]{2,1,0:T(8,128)(2,1)} %param.11) | copy-start | bytes 4718596
  193.6 3.8 %copy-start.10 = (bf16[1024,384]{0,1:T(8,128)(2,1)}, bf16[1024,384]{0,1:T(8,128)(2,1)S(1)}, u32[]{:S(2)}) copy-start(bf16[1024,384]{0,1:T(8,128)(2,1)S(1)} %get-tuple-element.15) | copy-start | bytes 2359300
  193.6 3.8 %copy-start.12 = (bf16[1024,384]{0,1:T(8,128)(2,1)}, bf16[1024,384]{0,1:T(8,128)(2,1)S(1)}, u32[]{:S(2)}) copy-start(bf16[1024,384]{0,1:T(8,128)(2,1)S(1)} %get-tuple-element.16) | copy-start | bytes 2359300
  193.7 4.4 %copy-start.4 = (bf16[1024,2048]{1,0:T(8,128)(2,1)S(1)}, bf16[1024,2048]{1,0:T(8,128)(2,1)}, u32[]{:S(2)}) copy-start(bf16[1024,2048]{1,0:T(8,128)(2,1)} %all-gather.3.cloned.1.call-done) | copy-start | bytes 12582916
  197.4 4.2 %copy-start.3 = (bf16[1024,2048]{1,0:T(8,128)(2,1)S(1)}, bf16[1024,2048]{1,0:T(8,128)(2,1)}, u32[]{:S(2)}) copy-start(bf16[1024,2048]{1,0:T(8,128)(2,1)} %all-gather.5.cloned.1.call-done) | copy-start | bytes 12582916
  197.5 7.4 %collective-permute-start.4 = (bf16[1024,2048]{1,0:T(8,128)(2,1)S(1)}, bf16[1024,2048]{1,0:T(8,128)(2,1)S(1)}, u32[]{:S(2)}, u32[]{:S(2)}) collective-permute-start(bf16[1024,2048]{1,0:T(8,128)(2,1)S(1)} %convolution_convert_fusion), channel_id=1, source_target_pairs={{0,16},{16,0},{1,17},{17,1},{2,18},{18,2},{3,19},{19,3},{4,20},{20... | collective-permute-start | bytes 12582920 | tf_op jit(solution)/shard_map/ppermute | solution.py:116
  201.7 2.6 copy-start.8
  210.0 6.9 %copy-start.11 = (bf16[1024,384]{0,1:T(8,128)(2,1)S(1)}, bf16[1024,384]{0,1:T(8,128)(2,1)}, u32[]{:S(2)}) copy-start(bf16[1024,384]{0,1:T(8,128)(2,1)} %copy-done.10) | copy-start | bytes 2359300
  210.0 6.9 %copy-start.13 = (bf16[1024,384]{0,1:T(8,128)(2,1)S(1)}, bf16[1024,384]{0,1:T(8,128)(2,1)}, u32[]{:S(2)}) copy-start(bf16[1024,384]{0,1:T(8,128)(2,1)} %copy-done.12) | copy-start | bytes 2359300
  216.9 5.5 %copy-start.5 = (bf16[1024,2048]{1,0:T(8,128)(2,1)S(1)}, bf16[1024,2048]{1,0:T(8,128)(2,1)}, u32[]{:S(2)}) copy-start(bf16[1024,2048]{1,0:T(8,128)(2,1)} %all-gather.3.cloned.1.call-done) | copy-start | bytes 12582916
  228.2 10.8 %all-to-all-start.1 = ((f32[16,1,128]{2,1,0:T(1,128)}), f32[16,1,128]{2,1,0:T(1,128)S(1)}, u32[]{:S(2)}, u32[]{:S(2)}) async-start(f32[16,1,128]{2,1,0:T(1,128)} %bitcast.9), calls=%async_computation.2 | async-start | bytes 16384 | tf_op jit(solution)/shard_map/all_to_all | solution.py:199
  239.0 64.7 %collective-permute-start.6 = (f32[16,1,128]{2,1,0:T(1,128)S(1)}, f32[16,1,128]{2,1,0:T(1,128)S(1)}, u32[]{:S(2)}, u32[]{:S(2)}) collective-permute-start(f32[16,1,128]{2,1,0:T(1,128)S(1)} %all-to-all-done.1), channel_id=1, source_target_pairs={{0,1},{1,0},{2,3},{3,2},{4,5},{5,4},{6,7},{7,6},{8,9},{9,8},{10,11... | collective-permute-start | bytes 24584 | tf_op jit(solution)/shard_map/ppermute | solution.py:116
  298.3 5.4 %copy-start.2 = (s32[128,8]{0,1:T(8,128)S(1)}, s32[128,8]{0,1:T(8,128)}, u32[]{:S(2)}) copy-start(s32[128,8]{0,1:T(8,128)} %param.9) | copy-start | bytes 12292
  298.3 7.8 %copy-start.1 = (bf16[128,2048]{1,0:T(8,128)(2,1)S(1)}, bf16[128,2048]{1,0:T(8,128)(2,1)}, u32[]{:S(2)}) copy-start(bf16[128,2048]{1,0:T(8,128)(2,1)} %reduce-scatter.2.cloned.1.call-done) | copy-start | bytes 1572868
  298.3 7.8 %collective-permute-start.5 = (bf16[128,1024]{1,0:T(8,128)(2,1)S(1)}, bf16[128,1024]{1,0:T(8,128)(2,1)S(1)}, u32[]{:S(2)}, u32[]{:S(2)}) collective-permute-start(bf16[128,1024]{1,0:T(8,128)(2,1)S(1)} %broadcast_select_fusion), channel_id=1, source_target_pairs={{0,1},{1,0},{2,3},{3,2},{4,5},{5,4},{6,7},{7,6},{8,9},{9,8},{10,11... | collective-permute-start | bytes 786440 | tf_op jit(solution)/shard_map/ppermute | solution.py:116
Sparse Core Ops, SparseCore 0:
  33.4 73.7 all-gather.2
  109.9 71.3 all-gather.4
  210.1 87.0 reduce-scatter.1
